TPU v7x, 32 devices: a whole 2x2x4 slice. The times are simulated.
32 devices in a mesh: seq: 8 (over z, x), chan: 4 (over y, core).
Axes of the slice: x: 2, y: 2, z: 4, core: 2. Of those that a mesh axis runs over, the one named last changes fastest.
Arguments:
- signal: float32 [256, 65536], P('chan', 'seq'), may hold values from -6 to 6
- gating: float32 [256, 65536], P('chan', 'seq'), may hold values from -6 to 6
- response: float32 [256, 65536], P('chan', 'seq'), may hold values from -0.0234375 to 0.0234375
- skip_gain: float32 [256], P('chan'), may hold values from -4 to 4
- mixing_weight: float32 [256, 256], P(None, 'chan'), may hold values from -0.5 to 0.5
Outputs:
- output: float32 [256, 65536], P('chan', 'seq')
All inputs are finite; a program needn't handle non-finite values.
Results may differ from a plain program's by a relative error of at most 0.00007.
Values sent between devices are 32-bit elements; how exact they have to be, the bound alone decides.
A program may use at most 128 MiB of HBM per device.

v0:
```python
from functools import partial
import math
import jax
import jax.numpy as jnp
import numpy as np
from jax import lax
from jax.sharding import PartitionSpec as P


def twiddle(number, period):
    angle = (number % period).astype(jnp.float32) * (2.0 * math.pi / period)
    return (jnp.cos(angle), jnp.sin(angle))


def rotate(real_part, imag_part, cos_part, sin_part):
    return (
        real_part * cos_part - imag_part * sin_part,
        imag_part * cos_part + real_part * sin_part,
    )


def dft_table(length, sign):
    steps = jnp.arange(length, dtype=jnp.int32)
    cos_part, sin_part = twiddle(steps[:, None] * steps[None, :], length)
    return (cos_part, sign * sin_part)


def complex_apply(pattern, table_real, table_imag, real_part, imag_part):
    contract = partial(jnp.einsum, pattern, precision=lax.Precision.HIGHEST)
    return (
        contract(table_real, real_part) - contract(table_imag, imag_part),
        contract(table_real, imag_part) + contract(table_imag, real_part),
    )


def spectral_order(length):
    if length <= 256:
        return np.arange(length)
    outer_len = length // 128
    return (spectral_order(outer_len)[:, None] + outer_len * np.arange(128)[None, :]).reshape(-1)


def whole_forward(real_part, imag_part, length):
    if length <= 256:
        table_real, table_imag = dft_table(length, -1.0)
        return complex_apply("kn,...n->...k", table_real, table_imag, real_part, imag_part)
    inner_len = 128
    outer_len = length // inner_len
    lead = real_part.shape[:-1]
    real_part = jnp.swapaxes(real_part.reshape(lead + (outer_len, inner_len)), -1, -2)
    imag_part = jnp.swapaxes(imag_part.reshape(lead + (outer_len, inner_len)), -1, -2)
    real_part, imag_part = whole_forward(real_part, imag_part, outer_len)
    real_part = jnp.swapaxes(real_part, -1, -2)
    imag_part = jnp.swapaxes(imag_part, -1, -2)
    freq_idx = jnp.asarray(spectral_order(outer_len), dtype=jnp.int32)[:, None]
    inner_idx = jnp.arange(inner_len, dtype=jnp.int32)[None, :]
    cos_part, sin_part = twiddle(freq_idx * inner_idx, length)
    real_part, imag_part = rotate(real_part, imag_part, cos_part, -sin_part)
    table_real, table_imag = dft_table(inner_len, -1.0)
    real_part, imag_part = complex_apply(
        "ub,...tb->...tu", table_real, table_imag, real_part, imag_part
    )
    return (real_part.reshape(lead + (length,)), imag_part.reshape(lead + (length,)))


def whole_inverse(real_part, imag_part, length):
    if length <= 256:
        table_real, table_imag = dft_table(length, 1.0)
        return complex_apply("kn,...n->...k", table_real, table_imag, real_part, imag_part)
    inner_len = 128
    outer_len = length // inner_len
    lead = real_part.shape[:-1]
    real_part = real_part.reshape(lead + (outer_len, inner_len))
    imag_part = imag_part.reshape(lead + (outer_len, inner_len))
    table_real, table_imag = dft_table(inner_len, 1.0)
    real_part, imag_part = complex_apply(
        "bu,...tu->...tb", table_real, table_imag, real_part, imag_part
    )
    freq_idx = jnp.asarray(spectral_order(outer_len), dtype=jnp.int32)[:, None]
    inner_idx = jnp.arange(inner_len, dtype=jnp.int32)[None, :]
    cos_part, sin_part = twiddle(freq_idx * inner_idx, length)
    real_part, imag_part = rotate(real_part, imag_part, cos_part, sin_part)
    real_part, imag_part = whole_inverse(
        jnp.swapaxes(real_part, -1, -2), jnp.swapaxes(imag_part, -1, -2), outer_len
    )
    real_part = jnp.swapaxes(real_part, -1, -2)
    imag_part = jnp.swapaxes(imag_part, -1, -2)
    return (real_part.reshape(lead + (length,)), imag_part.reshape(lead + (length,)))


def owner_conv(stacked, groups, samples):
    chan_rows = stacked.shape[1]
    own_rows = chan_rows // groups
    span = groups * samples
    pieces = stacked.reshape(2, groups, own_rows, samples)
    rows_whole = lax.all_to_all(pieces, "seq", split_axis=1, concat_axis=3, tiled=True).reshape(
        2, own_rows, span
    )
    padded = jnp.concatenate([rows_whole, jnp.zeros_like(rows_whole)], axis=2)
    spec_real, spec_imag = whole_forward(padded, jnp.zeros_like(padded), 2 * span)
    prod_real = spec_real[0] * spec_real[1] - spec_imag[0] * spec_imag[1]
    prod_imag = spec_real[0] * spec_imag[1] + spec_imag[0] * spec_real[1]
    back_real, back_imag = whole_inverse(prod_real, prod_imag, 2 * span)
    conv_rows = back_real[:, :span]
    return lax.all_to_all(conv_rows, "seq", split_axis=1, concat_axis=0, tiled=True)


def per_device(signal, gating, response, skip_gain, mixing_weight):
    chan_rows, samples = signal.shape
    groups = lax.axis_size("seq")
    full_len = 2 * groups * samples
    stacked = jnp.stack([signal, response])
    conv = owner_conv(stacked, groups, samples)
    conv = conv / full_len
    mixed_in = gating * (conv + skip_gain[:, None] * signal)
    return lax.psum_scatter(
        jnp.dot(
            mixing_weight,
            mixed_in,
            precision=lax.Precision.HIGHEST,
            preferred_element_type=jnp.float32,
        ),
        "chan",
        scatter_dimension=0,
        tiled=True,
    )


def solution(mesh):
    in_specs = (P("chan", "seq"), P("chan", "seq"), P("chan", "seq"), P("chan"), P(None, "chan"))
    out_specs = P("chan", "seq")
    return jax.shard_map(
        per_device, mesh=mesh, in_specs=in_specs, out_specs=out_specs, check_vma=False
    )
```

profile of v0, /device:TPU:0, one launch (start us, length us, event | category | flops | bytes accessed | tf_op | source)
XLA Modules:
  0.0 486.4 jit_solution(6807660299492079792)
XLA Ops:
  6.5 0.0 copy-start
  6.5 4.6 pad_maximum_fusion
  11.1 0.0 copy-start.7
  11.1 7.4 %all-to-all-start = ((f32[2,8,8,8192]{3,2,0,1:T(8,128)}), f32[2,8,8,8192]{3,2,0,1:T(8,128)}, u32[]{:S(2)}, u32[]{:S(2)}) async-start(f32[2,8,8,8192]{3,2,0,1:T(8,128)} %pad_maximum_fusion), calls=%async_computation | async-start | bytes 8388608 | tf_op jit(solution)/shard_map/all_to_all | solution.py:96
  18.6 0.0 reduce-scatter.4.cloned.1.call-start
  18.6 0.1 sine_negate_fusion.1
  18.7 0.1 fusion.149
  18.7 0.0 copy-done.7
  18.7 2.1 fusion.70
  20.8 3.4 fusion.69
  24.3 8.9 %fusion.34 = f32[2,8,128,128,8]{3,4,2,1,0:T(8,128)} fusion(), kind=kOutput, calls=%fused_computation.58 | convolution fusion | flops 201327552 | bytes 8388608 | tf_op jit(solution)/shard_map/kn,...n->...k/dot_general | solution.py:31
  33.2 78.7 %all-to-all-done = f32[2,8,8,8192]{3,2,0,1:T(8,128)} async-done(((f32[2,8,8,8192]{3,2,0,1:T(8,128)}), f32[2,8,8,8192]{3,2,0,1:T(8,128)}, u32[]{:S(2)}, u32[]{:S(2)}) %all-to-all-start) | async-done | bytes 4194336 | tf_op jit(solution)/shard_map/all_to_all | solution.py:96
  111.8 6.6 %copy.47 = f32[2,1,8,8,8192]{4,3,2,0,1:T(8,128)} copy(f32[2,1,8,8,8192]{4,2,0,3,1:T(8,128)} %bitcast.3) | data formatting | bytes 8388608 | tf_op jit(solution)/shard_map/all_to_all | solution.py:96
  118.4 4.0 reshape.255
  122.4 2.7 pad_bitcast_fusion
  125.1 4.9 %copy.100 = f32[2,8,1024,128]{3,2,1,0:T(8,128)} copy(f32[2,8,1024,128]{3,1,2,0:T(8,128)S(1)} %pad_bitcast_fusion) | data formatting | bytes 16777216
  130.0 8.7 %copy.74 = f32[2,8,128,8,128]{4,3,2,1,0:T(8,128)} copy(f32[2,8,128,8,128]{2,4,3,1,0:T(8,128)} %bitcast.216) | data formatting | bytes 16777216 | tf_op jit(solution)/shard_map/reshape | solution.py:50
  138.6 12.5 %fusion.4 = f32[2,8,128,128,8]{3,4,2,1,0:T(8,128)} fusion(f32[2,8,128,8,128]{4,3,2,1,0:T(8,128)} %copy.74), kind=kOutput, calls=%fused_computation.14 | convolution fusion | flops 201327552 | bytes 16777216 | tf_op jit(solution)/shard_map/kn,...n->...k/dot_general | solution.py:32
  151.1 0.0 copy-done.1
  151.1 9.3 %fusion.6 = f32[2,8,128,128,8]{3,4,2,1,0:T(8,128)} fusion(f32[2,8,128,8,128]{4,3,2,1,0:T(8,128)S(1)} %copy-done.1), kind=kOutput, calls=%fused_computation.16 | convolution fusion | flops 201327488 | bytes 16777216 | tf_op jit(solution)/shard_map/kn,...n->...k/dot_general | solution.py:31
  160.4 15.3 %fusion.2 = (f32[2,8,128,8,128]{4,3,2,1,0:T(8,128)}, f32[2,8,128,8,128]{4,3,2,1,0:T(8,128)S(1)}) fusion(f32[8,128]{1,0:T(8,128)S(1)} %get-tuple-element.19, f32[8,128]{1,0:T(8,128)S(1)} %get-tuple-element.20, f32[2,8,128,128,8]{3,4,2,1,0:T(8,128)} %fusion.4, f32[2,8,128,128,8]{3,4,2,1,0:T(8,128)} %fusion.6, f32[2,8,128,128,8]{3,4,2,1,0:T(8,128)} %fusion.34), kind=kOutput, calls=%fused_computation.10 | convolution fusion | flops 218104704 | bytes 41951232 | tf_op jit(solution)/shard_map/kn,...n->...k/dot_general | solution.py:32
  175.7 11.1 %fusion.8 = f32[2,8,128,8,128]{2,4,3,1,0:T(8,128)} fusion(f32[2,8,128,8,128]{4,3,2,1,0:T(8,128)S(1)} %get-tuple-element.6), kind=kOutput, calls=%fused_computation.19 | convolution fusion | flops 3221454848 | bytes 16777216 | tf_op jit(solution)/shard_map/ub,...tb->...tu/dot_general | solution.py:32
  186.8 0.0 slice-start.1
  186.8 8.8 %fusion.10 = f32[2,8,128,8,128]{2,4,3,1,0:T(8,128)S(1)} fusion(f32[2,8,128,8,128]{4,3,2,1,0:T(8,128)S(1)} %get-tuple-element.6), kind=kOutput, calls=%fused_computation.21 | convolution fusion | flops 3221471232 | bytes 16777216 | tf_op jit(solution)/shard_map/ub,...tb->...tu/dot_general | solution.py:31
  195.7 0.0 slice-done
  195.7 0.0 slice-done.1
  195.7 13.0 %fusion.39 = f32[2,8,128,8,128]{2,4,3,1,0:T(8,128)} fusion(f32[2,8,128,8,128]{2,4,3,1,0:T(8,128)} %fusion.8, f32[2,8,128,8,128]{4,3,2,1,0:T(8,128)S(1)} %bitcast.211), kind=kOutput, calls=%fused_computation.61 | convolution fusion | flops 3223568384 | bytes 25165824 | tf_op jit(solution)/shard_map/ub,...tb->...tu/dot_general | solution.py:32
  208.7 10.7 %fusion.36 = f32[2,8,128,8,128]{2,4,3,1,0:T(8,128)} fusion(f32[2,8,128,8,128]{2,4,3,1,0:T(8,128)S(1)} %fusion.10, f32[2,8,128,8,128]{4,3,2,1,0:T(8,128)S(1)} %bitcast.211), kind=kOutput, calls=%fused_computation.60 | convolution fusion | flops 3223552000 | bytes 25165824 | tf_op jit(solution)/shard_map/ub,...tb->...tu/dot_general | solution.py:31
  219.4 7.0 %fusion = (f32[2,8,1024,128]{3,2,1,0:T(8,128)S(1)}, f32[2,8,1024,128]{3,2,1,0:T(8,128)S(1)}) fusion(f32[2,8,128,8,128]{2,4,3,1,0:T(8,128)} %fusion.36, f32[2,8,128,8,128]{2,4,3,1,0:T(8,128)} %fusion.39, f32[1024,128]{1,0:T(8,128)S(1)} %get-tuple-element.18, f32[1024,128]{1,0:T(8,128)S(1)} %get-tuple-element.17), kind=kLoop, calls=%fused_computation.4 | loop fusion | flops 12582912 | bytes 34603008 | tf_op jit(solution)/shard_map/sub | solution.py:17
  226.5 9.7 %fusion.88 = f32[2,8,1024,128]{3,2,1,0:T(8,128)} fusion(f32[2,8,1024,128]{3,2,1,0:T(8,128)S(1)} %get-tuple-element.7), kind=kOutput, calls=%fused_computation.116 | convolution fusion | flops 3221454848 | bytes 16777216 | tf_op jit(solution)/shard_map/ub,...tb->...tu/dot_general | solution.py:31
  236.2 7.8 %fusion.86 = f32[2,8,1024,128]{3,2,1,0:T(8,128)S(1)} fusion(f32[2,8,1024,128]{3,2,1,0:T(8,128)S(1)} %get-tuple-element.8), kind=kOutput, calls=%fused_computation.114 | convolution fusion | flops 3221454848 | bytes 16777216 | tf_op jit(solution)/shard_map/ub,...tb->...tu/dot_general | solution.py:32
  244.0 11.4 %convolution_subtract_fusion = f32[2,8,1024,128]{3,2,1,0:T(8,128)} fusion(f32[2,8,1024,128]{3,2,1,0:T(8,128)} %fusion.88, f32[2,8,1024,128]{3,2,1,0:T(8,128)S(1)} %get-tuple-element.8), kind=kOutput, calls=%fused_computation.63 | convolution fusion | flops 3223568384 | bytes 25165824 | tf_op jit(solution)/shard_map/ub,...tb->...tu/dot_general | solution.py:31
  255.4 9.5 %convolution_add_fusion = f32[2,8,1024,128]{3,2,1,0:T(8,128)} fusion(f32[2,8,1024,128]{3,2,1,0:T(8,128)S(1)} %fusion.86, f32[2,8,1024,128]{3,2,1,0:T(8,128)S(1)} %get-tuple-element.7), kind=kOutput, calls=%fused_computation.62 | convolution fusion | flops 3223568384 | bytes 25165824 | tf_op jit(solution)/shard_map/ub,...tb->...tu/dot_general | solution.py:32
  264.9 0.0 copy-done.2
  264.9 4.2 multiply_subtract_fusion
  269.1 3.8 fusion.22
  272.9 3.8 fusion.20
  276.8 0.0 copy-start.4
  276.8 0.0 copy-start.5
  276.8 3.8 fusion.44
  280.6 0.0 copy-done.4
  280.6 0.0 copy-done.5
  280.6 5.2 %fusion.18 = (f32[8,128,1024]{1,2,0:T(8,128)S(1)}, f32[8,128,1024]{1,2,0:T(8,128)S(1)}) fusion(f32[8,1024,128]{2,1,0:T(8,128)S(1)} %fusion.44, f32[128,1024]{0,1:T(8,128)S(1)} %copy-done.5, f32[128,1024]{0,1:T(8,128)S(1)} %copy-done.4, f32[8,1024,128]{2,1,0:T(8,128)S(1)} %fusion.20, f32[1,8,1024,128]{3,2,1,0:T(8,128)S(1)} %get-tuple-element.9), kind=kOutput, calls=%fused_computation.37 | convolution fusion | flops 1618182144 | bytes 22020096 | tf_op jit(solution)/shard_map/bu,...tu->...tb/dot_general | solution.py:32
  285.9 7.0 %fusion.84 = f32[8,128,8,128]{3,1,2,0:T(8,128)S(1)} fusion(f32[8,128,8,128]{1,3,2,0:T(8,128)S(1)} %bitcast.212), kind=kOutput, calls=%fused_computation.112 | convolution fusion | flops 1610842112 | bytes 8388608 | tf_op jit(solution)/shard_map/bu,...tu->...tb/dot_general | solution.py:31
  292.9 7.3 %fusion.82 = f32[8,128,8,128]{3,1,2,0:T(8,128)S(1)} fusion(f32[8,128,8,128]{1,3,2,0:T(8,128)S(1)} %bitcast.214), kind=kOutput, calls=%fused_computation.110 | convolution fusion | flops 1610842112 | bytes 8388608 | tf_op jit(solution)/shard_map/bu,...tu->...tb/dot_general | solution.py:32
  300.2 7.1 %convolution_subtract_fusion.1 = f32[8,128,8,128]{3,1,2,0:T(8,128)S(1)} fusion(f32[8,128,8,128]{3,1,2,0:T(8,128)S(1)} %fusion.84, f32[8,128,8,128]{1,3,2,0:T(8,128)S(1)} %bitcast.215), kind=kOutput, calls=%fused_computation.67 | convolution fusion | flops 1611890688 | bytes 12582912 | tf_op jit(solution)/shard_map/bu,...tu->...tb/dot_general | solution.py:31
  307.3 7.3 %fusion.16 = (f32[8,128,128,8]{2,1,3,0:T(8,128)S(1)}, f32[8,128,128,8]{2,1,3,0:T(8,128)S(1)}) fusion(f32[8,128,8,128]{3,1,2,0:T(8,128)S(1)} %convolution_subtract_fusion.1, f32[128,8]{0,1:T(8,128)S(1)} %get-tuple-element.21, f32[128,8]{0,1:T(8,128)S(1)} %get-tuple-element.22, f32[8,128,8,128]{3,1,2,0:T(8,128)S(1)} %fusion.82, ...), kind=kOutput, calls=%fused_computation.31 | convolution fusion | flops 1618182144 | bytes 20979712 | tf_op jit(solution)/shard_map/bu,...tu->...tb/dot_general | solution.py:32
  314.6 6.6 %fusion.28 = f32[8,128,128,8]{2,3,1,0:T(8,128)S(1)} fusion(f32[8,128,128,8]{2,1,3,0:T(8,128)S(1)} %get-tuple-element.14), kind=kOutput, calls=%fused_computation.49 | convolution fusion | flops 100664192 | bytes 8388608 | tf_op jit(solution)/shard_map/kn,...n->...k/dot_general | solution.py:31
  321.2 6.9 %subtract_bitcast_fusion = f32[8,128,8,128]{3,2,1,0:T(8,128)} fusion(f32[8,128,128,8]{2,3,1,0:T(8,128)S(1)} %fusion.28, f32[8,128,128,8]{2,1,3,0:T(8,128)S(1)} %get-tuple-element.13), kind=kOutput, calls=%fused_computation.53 | convolution fusion | flops 101712768 | bytes 12582912 | tf_op jit(solution)/shard_map/kn,...n->...k/dot_general | solution.py:31
  328.1 5.4 %copy.75 = f32[8,128,8,128]{1,3,2,0:T(8,128)} copy(f32[8,128,8,128]{3,2,1,0:T(8,128)} %subtract_bitcast_fusion) | data formatting | bytes 8388608 | tf_op jit(solution)/shard_map/reshape | solution.py:88
  333.5 4.6 copy.101
  338.1 0.0 copy-start.3
  338.1 0.0 copy-start.6
  338.1 0.0 copy-start.8
  338.1 0.1 slice.32
  338.3 52.3 %all_to_all.28 = f32[8,8,8192]{2,0,1:T(8,128)S(1)} all-to-all(f32[8,8,8192]{2,0,1:T(8,128)S(1)} %bitcast.219), channel_id=1, replica_groups=mesh['seq'=8,'chan'=4] {'seq'}, dimensions={1} | all-to-all | bytes 4194304 | tf_op jit(solution)/shard_map/all_to_all | solution.py:105
  390.6 0.0 copy-done
  390.6 0.0 copy-done.3
  390.6 0.0 copy-done.6
  390.6 0.0 copy-done.8
  390.6 9.1 %convolution_bitcast_fusion = f32[256,8192]{0,1:T(8,128)} fusion(f32[256,64]{0,1:T(8,128)S(1)} %copy-done, f32[64,8192]{1,0:T(8,128)S(1)} %copy-done.6, f32[64,8192]{1,0:T(8,128)S(1)} %copy-done.3, f32[8,8,8192]{2,0,1:T(8,128)S(1)} %all_to_all.28, f32[64]{0:T(128)S(1)} %copy-done.8), kind=kOutput, calls=%fused_computation | convolution fusion | flops 1612709888 | bytes 14745856 | tf_op jit(solution)/shard_map/dot_general | solution.py:117
  399.7 8.9 %copy.76 = f32[256,8192]{1,0:T(8,128)} copy(f32[256,8192]{0,1:T(8,128)} %convolution_bitcast_fusion) | data formatting | bytes 16777216
  408.6 0.0 reduce-scatter.4.cloned.1.call-update
  408.6 70.6 %reduce-scatter.4.cloned.1.call-done = f32[64,8192]{1,0:T(8,128)} async-done(((f32[256,8192]{1,0:T(8,128)}), f32[64,8192]{1,0:T(8,128)}) %reduce-scatter.4.cloned.1.call-update) | async-done | bytes 2097168 | tf_op jit(solution)/shard_map/reduce_scatter | solution.py:116
  (4 shorter events, 0.0 us)
Async XLA Ops:
  6.5 384.1 %copy-start = (f32[256,64]{0,1:T(8,128)S(1)}, f32[256,64]{0,1:T(8,128)}, u32[]{:S(2)}) copy-start(f32[256,64]{0,1:T(8,128)} %param.13) | copy-start | bytes 196612
  11.1 7.6 %copy-start.7 = (s32[1024]{0:T(1024)S(1)}, s32[1024]{0:T(1024)}, u32[]{:S(2)}) copy-start(s32[1024]{0:T(1024)} %constant.100.clone) | copy-start | bytes 12292
  11.1 100.7 %all-to-all-start = ((f32[2,8,8,8192]{3,2,0,1:T(8,128)}), f32[2,8,8,8192]{3,2,0,1:T(8,128)}, u32[]{:S(2)}, u32[]{:S(2)}) async-start(f32[2,8,8,8192]{3,2,0,1:T(8,128)} %pad_maximum_fusion), calls=%async_computation | async-start | bytes 8388608 | tf_op jit(solution)/shard_map/all_to_all | solution.py:96
  18.6 460.7 %reduce-scatter.4.cloned.1.call-start = ((), (), s32[]{:S(2)}) async-start(), calls=%async_computation.3 | async-start | bytes 10485760 | tf_op jit(solution)/shard_map/reduce_scatter | solution.py:116
  138.6 12.5 %copy-start.1 = (f32[2,8,128,8,128]{4,3,2,1,0:T(8,128)S(1)}, f32[2,8,128,8,128]{4,3,2,1,0:T(8,128)}, u32[]{:S(2)}) copy-start(f32[2,8,128,8,128]{4,3,2,1,0:T(8,128)} %copy.74) | copy-start | bytes 25165828
  175.7 20.0 %slice-start = ((s8[8388608]{0:T(1024)(128)(4,1)}), s8[4194304]{0:T(1024)(128)(4,1)S(1)}, s32[]{:S(2)}) async-start(s8[8388608]{0:T(1024)(128)(4,1)} %bitcast.210), calls=%async_computation.4 | async-start | bytes 8388608
  186.8 8.9 %slice-start.1 = ((s8[8388608]{0:T(1024)(128)(4,1)}), s8[4194304]{0:T(1024)(128)(4,1)S(1)}, s32[]{:S(2)}) async-start(s8[8388608]{0:T(1024)(128)(4,1)} %bitcast.210), calls=%async_computation.5 | async-start | bytes 8388608
  255.4 9.5 %copy-start.2 = (f32[2,8,1024,128]{3,2,1,0:T(8,128)S(1)}, f32[2,8,1024,128]{3,2,1,0:T(8,128)}, u32[]{:S(2)}) copy-start(f32[2,8,1024,128]{3,2,1,0:T(8,128)} %convolution_subtract_fusion) | copy-start | bytes 25165828
  276.8 3.9 copy-start.4
  276.8 3.9 copy-start.5
  338.1 52.5 %copy-start.3 = (f32[64,8192]{1,0:T(8,128)S(1)}, f32[64,8192]{1,0:T(8,128)}, u32[]{:S(2)}) copy-start(f32[64,8192]{1,0:T(8,128)} %param.9) | copy-start | bytes 6291460
  338.1 52.5 %copy-start.6 = (f32[64,8192]{1,0:T(8,128)S(1)}, f32[64,8192]{1,0:T(8,128)}, u32[]{:S(2)}) copy-start(f32[64,8192]{1,0:T(8,128)} %param.10) | copy-start | bytes 6291460
  338.1 52.5 %copy-start.8 = (f32[64]{0:T(128)S(1)}, f32[64]{0:T(128)}, u32[]{:S(2)}) copy-start(f32[64]{0:T(128)} %param.12) | copy-start | bytes 772
Sparse Core Ops, SparseCore 0:
  408.8 70.4 reduce-scatter.3
where the time goes:
time: 490 us; the launch traced here: 486 us
  matrix products  196 us (40%)
  waiting for transfers between devices  149 us (30%)
  blocking collectives  52.3 us (11%)
  local copies, waits for them, and re-layouts  45.9 us (9%)
  other arithmetic  21.5 us (4%)
  between operations  13.9 us (3%)
  starting transfers between devices  7.45 us (2%)
    all_to_all x1, waiting for transfers between devices, owner_conv(): lax.all_to_all(pieces, 'seq', split_axis=1, concat_axis=3, tiled=True)  78.7 us
    reduce_scatter x1, waiting for transfers between devices, per_device(): lax.psum_scatter(jnp.dot(mixing_weight, mixed_in, precision=lax.Precision...  70.6 us
    all_to_all x1, blocking collectives, owner_conv(): lax.all_to_all(conv_rows, 'seq', split_axis=1, concat_axis=0, tiled=True)  52.3 us
    dot_general x5, matrix products, complex_apply(): contract(table_imag, real_part)  47.6 us
    dot_general x6, matrix products, complex_apply(): contract(table_real, real_part) - contract(table_imag, imag_part)  47.5 us
    dot_general x6, matrix products, complex_apply(): contract(table_imag, imag_part)  46.6 us
    dot_general x5, matrix products, complex_apply(): contract(table_real, imag_part) + contract(table_imag, real_part)  45.3 us
    unnamed x26, local copies, waits for them, and re-layouts  21.2 us
  transfers between devices with their start and end apart: 2, of which 2 were waited for; matrix products, arithmetic and copies ran while one was open for 3% of the time, Pallas kernels for 0%

commit v1 on v0

--- a/solution.py
+++ b/solution.py
@@ -5,6 +5,22 @@
 import numpy as np
 from jax import lax
 from jax.sharding import PartitionSpec as P
+
+
+def exchange_in_pairs(x, axis, split, join):
+    ways, here = (lax.axis_size(axis), lax.axis_index(axis))
+    width = x.shape[split] // ways
+    shape = list(x.shape)
+    shape[split] = width
+    height = shape[join]
+    shape[join] = height * ways
+    full = jnp.zeros(shape, x.dtype)
+    for mask in range(ways):
+        part = lax.dynamic_slice_in_dim(x, (here ^ mask) * width, width, axis=split)
+        if mask:
+            part = lax.ppermute(part, axis, [(d, d ^ mask) for d in range(ways)])
+        full = lax.dynamic_update_slice_in_dim(full, part, (here ^ mask) * height, axis=join)
+    return full
 
 
 def twiddle(number, period):
@@ -93,9 +109,7 @@
     own_rows = chan_rows // groups
     span = groups * samples
     pieces = stacked.reshape(2, groups, own_rows, samples)
-    rows_whole = lax.all_to_all(pieces, "seq", split_axis=1, concat_axis=3, tiled=True).reshape(
-        2, own_rows, span
-    )
+    rows_whole = exchange_in_pairs(pieces, "seq", 1, 3).reshape(2, own_rows, span)
     padded = jnp.concatenate([rows_whole, jnp.zeros_like(rows_whole)], axis=2)
     spec_real, spec_imag = whole_forward(padded, jnp.zeros_like(padded), 2 * span)
     prod_real = spec_real[0] * spec_real[1] - spec_imag[0] * spec_imag[1]

time: 490 us -> 473 us (0.965)
  waiting for transfers between devices: 149 us -> 113 us
  blocking collectives: 52.3 us -> 70.2 us
  starting transfers between devices: 7.45 us -> 13.4 us
  local copies, waits for them, and re-layouts: 45.9 us -> 40.4 us
    all_to_all x1 -> x0, waiting for transfers between devices: 78.7 us -> none  [owner_conv(): lax.all_to_all(pieces, 'seq', split_axis=1, concat_axis=3, tiled=True)]
    ppermute x0 -> x7, waiting for transfers between devices: none -> 42.3 us  [exchange_in_pairs(): part = lax.ppermute(part, axis, [(d, d ^ mask) for d in range(ways)])]
    all_to_all x1, blocking collectives: 52.3 us -> 70.2 us  [owner_conv(): lax.all_to_all(conv_rows, 'seq', split_axis=1, concat_axis=0, tiled=True)]
    ppermute x0 -> x7, starting transfers between devices: none -> 13.4 us  [exchange_in_pairs(): part = lax.ppermute(part, axis, [(d, d ^ mask) for d in range(ways)])]
    all_to_all x1 -> x0, starting transfers between devices: 7.41 us -> none  [owner_conv(): lax.all_to_all(pieces, 'seq', split_axis=1, concat_axis=3, tiled=True)]
    all_to_all x1 -> x0, local copies, waits for them, and re-layouts: 6.56 us -> none  [owner_conv(): lax.all_to_all(pieces, 'seq', split_axis=1, concat_axis=3, tiled=True)]
    dynamic_update_slice x0 -> x7, local copies, waits for them, and re-layouts: none -> 5.47 us  [exchange_in_pairs(): lax.dynamic_update_slice_in_dim(full, part, (here ^ mask) * height, axis=...]
    unnamed x26 -> x34, local copies, waits for them, and re-layouts: 21.2 us -> 20.4 us
  transfers between devices with their start and end apart: 2 -> 8, of which waited for: 2 -> 4; matrix products, arithmetic and copies ran while one was open for 3% -> 5% of each run, Pallas kernels for 0% -> 0%
where the time goes in v1:
time: 473 us; the launch traced here: 469 us
  matrix products  196 us (41%)
  waiting for transfers between devices  113 us (24%)
  blocking collectives  70.2 us (15%)
  local copies, waits for them, and re-layouts  40.4 us (9%)
  other arithmetic  22.4 us (5%)
  between operations  14 us (3%)
  starting transfers between devices  13.4 us (3%)
    reduce_scatter x1, waiting for transfers between devices, per_device(): lax.psum_scatter(jnp.dot(mixing_weight, mixed_in, precision=lax.Precision...  70.6 us
    all_to_all x1, blocking collectives, owner_conv(): lax.all_to_all(conv_rows, 'seq', split_axis=1, concat_axis=0, tiled=True)  70.2 us
    dot_general x6, matrix products, complex_apply(): contract(table_real, real_part) - contract(table_imag, imag_part)  47.8 us
    dot_general x5, matrix products, complex_apply(): contract(table_imag, real_part)  47.4 us
    dot_general x6, matrix products, complex_apply(): contract(table_imag, imag_part)  46.6 us
    dot_general x5, matrix products, complex_apply(): contract(table_real, imag_part) + contract(table_imag, real_part)  45 us
    ppermute x7, waiting for transfers between devices, exchange_in_pairs(): part = lax.ppermute(part, axis, [(d, d ^ mask) for d in range(ways)])  42.3 us
    unnamed x34, local copies, waits for them, and re-layouts  20.4 us
  transfers between devices with their start and end apart: 8, of which 4 were waited for; matrix products, arithmetic and copies ran while one was open for 5% of the time, Pallas kernels for 0%

profile of v1, /device:TPU:0, one launch (start us, length us, event | category | flops | bytes accessed | tf_op | source)
XLA Modules:
  0.0 469.1 jit_solution(389231470516018859)
XLA Ops:
  6.5 3.7 fusion.62
  10.3 3.0 collective-permute-start
  13.2 1.6 collective-permute-start.1
  14.8 3.0 collective-permute-start.3
  17.8 1.3 collective-permute-start.4
  19.1 0.1 sine_negate_fusion.1
  19.1 0.1 fusion.175
  19.2 1.8 fusion.71
  21.0 2.1 fusion.80
  23.1 0.0 copy-start.5
  23.2 0.3 reshape.286
  23.4 1.3 copy-done.5
  24.8 3.4 fusion.79
  28.2 8.9 %fusion.34 = f32[2,8,128,128,8]{3,4,2,1,0:T(8,128)} fusion(), kind=kOutput, calls=%fused_computation.73 | convolution fusion | flops 201327552 | bytes 8388608 | tf_op jit(solution)/shard_map/kn,...n->...k/dot_general | solution.py:47
  37.1 3.6 collective-permute-start.5
  40.7 1.1 bitcast_dynamic-update-slice_fusion.6
  41.8 8.2 %collective-permute-done.1 = f32[2,1,8,8192]{3,2,0,1:T(8,128)} collective-permute-done((f32[2,1,8,8192]{3,2,0,1:T(8,128)}, f32[2,1,8,8192]{3,2,0,1:T(8,128)}, u32[]{:S(2)}, u32[]{:S(2)}) %collective-permute-start.1) | collective-permute-done | bytes 524320 | tf_op jit(solution)/shard_map/ppermute | solution.py:21
  50.0 0.9 collective-permute-start.6
  50.9 1.1 bitcast_dynamic-update-slice_fusion.5
  52.0 6.9 %collective-permute-done.2 = f32[2,1,8,8192]{3,2,0,1:T(8,128)} collective-permute-done((f32[2,1,8,8192]{3,2,0,1:T(8,128)}, f32[2,1,8,8192]{3,2,0,1:T(8,128)}, u32[]{:S(2)}, u32[]{:S(2)}) %collective-permute-start.2) | collective-permute-done | bytes 524320 | tf_op jit(solution)/shard_map/ppermute | solution.py:21
  58.9 1.1 bitcast_dynamic-update-slice_fusion.4
  60.0 1.1 bitcast_dynamic-update-slice_fusion.3
  61.0 27.3 %collective-permute-done.4 = f32[2,1,8,8192]{3,2,0,1:T(8,128)} collective-permute-done((f32[2,1,8,8192]{3,2,0,1:T(8,128)}, f32[2,1,8,8192]{3,2,0,1:T(8,128)}, u32[]{:S(2)}, u32[]{:S(2)}) %collective-permute-start.4) | collective-permute-done | bytes 524320 | tf_op jit(solution)/shard_map/ppermute | solution.py:21
  88.3 1.1 bitcast_dynamic-update-slice_fusion.2
  89.4 0.0 collective-permute-done.5
  89.5 0.0 collective-permute-done.6
  89.5 0.5 pad_bitcast_fusion
  90.1 4.9 %copy.90 = f32[2,8,1024,128]{3,2,1,0:T(8,128)} copy(f32[2,8,1024,128]{3,1,2,0:T(8,128)S(1)} %pad_bitcast_fusion) | data formatting | bytes 16777216
  95.0 8.7 %copy.64 = f32[2,8,128,8,128]{4,3,2,1,0:T(8,128)} copy(f32[2,8,128,8,128]{2,4,3,1,0:T(8,128)} %bitcast.234) | data formatting | bytes 16777216 | tf_op jit(solution)/shard_map/reshape | solution.py:66
  103.7 12.3 %fusion.4 = f32[2,8,128,128,8]{3,4,2,1,0:T(8,128)} fusion(f32[2,8,128,8,128]{4,3,2,1,0:T(8,128)} %copy.64), kind=kOutput, calls=%fused_computation.30 | convolution fusion | flops 201327552 | bytes 16777216 | tf_op jit(solution)/shard_map/kn,...n->...k/dot_general | solution.py:48
  115.9 9.5 %fusion.6 = f32[2,8,128,128,8]{3,4,2,1,0:T(8,128)} fusion(f32[2,8,128,8,128]{4,3,2,1,0:T(8,128)S(1)} %copy-done.1), kind=kOutput, calls=%fused_computation.32 | convolution fusion | flops 201327488 | bytes 16777216 | tf_op jit(solution)/shard_map/kn,...n->...k/dot_general | solution.py:47
  125.4 15.1 %fusion.2 = (f32[2,8,128,8,128]{4,3,2,1,0:T(8,128)}, f32[2,8,128,8,128]{4,3,2,1,0:T(8,128)S(1)}) fusion(f32[8,128]{1,0:T(8,128)S(1)} %get-tuple-element.25, f32[8,128]{1,0:T(8,128)S(1)} %get-tuple-element.26, f32[2,8,128,128,8]{3,4,2,1,0:T(8,128)} %fusion.4, f32[2,8,128,128,8]{3,4,2,1,0:T(8,128)} %fusion.6, f32[2,8,128,128,8]{3,4,2,1,0:T(8,128)} %fusion.34), kind=kOutput, calls=%fused_computation.26 | convolution fusion | flops 218104704 | bytes 41951232 | tf_op jit(solution)/shard_map/kn,...n->...k/dot_general | solution.py:48
  140.5 11.0 %fusion.8 = f32[2,8,128,8,128]{2,4,3,1,0:T(8,128)} fusion(f32[2,8,128,8,128]{4,3,2,1,0:T(8,128)S(1)} %get-tuple-element.6), kind=kOutput, calls=%fused_computation.35 | convolution fusion | flops 3221454848 | bytes 16777216 | tf_op jit(solution)/shard_map/ub,...tb->...tu/dot_general | solution.py:48
  151.6 0.0 slice-start.1
  151.6 8.8 %fusion.10 = f32[2,8,128,8,128]{2,4,3,1,0:T(8,128)S(1)} fusion(f32[2,8,128,8,128]{4,3,2,1,0:T(8,128)S(1)} %get-tuple-element.6), kind=kOutput, calls=%fused_computation.37 | convolution fusion | flops 3221471232 | bytes 16777216 | tf_op jit(solution)/shard_map/ub,...tb->...tu/dot_general | solution.py:47
  160.4 13.0 %fusion.39 = f32[2,8,128,8,128]{2,4,3,1,0:T(8,128)} fusion(f32[2,8,128,8,128]{2,4,3,1,0:T(8,128)} %fusion.8, f32[2,8,128,8,128]{4,3,2,1,0:T(8,128)S(1)} %bitcast.226), kind=kOutput, calls=%fused_computation.76 | convolution fusion | flops 3223568384 | bytes 25165824 | tf_op jit(solution)/shard_map/ub,...tb->...tu/dot_general | solution.py:48
  173.5 10.7 %fusion.36 = f32[2,8,128,8,128]{2,4,3,1,0:T(8,128)} fusion(f32[2,8,128,8,128]{2,4,3,1,0:T(8,128)S(1)} %fusion.10, f32[2,8,128,8,128]{4,3,2,1,0:T(8,128)S(1)} %bitcast.226), kind=kOutput, calls=%fused_computation.75 | convolution fusion | flops 3223552000 | bytes 25165824 | tf_op jit(solution)/shard_map/ub,...tb->...tu/dot_general | solution.py:47
  184.2 7.0 %fusion = (f32[2,8,1024,128]{3,2,1,0:T(8,128)S(1)}, f32[2,8,1024,128]{3,2,1,0:T(8,128)S(1)}) fusion(f32[2,8,128,8,128]{2,4,3,1,0:T(8,128)} %fusion.36, f32[2,8,128,8,128]{2,4,3,1,0:T(8,128)} %fusion.39, f32[1024,128]{1,0:T(8,128)S(1)} %get-tuple-element.24, f32[1024,128]{1,0:T(8,128)S(1)} %get-tuple-element.23), kind=kLoop, calls=%fused_computation.20 | loop fusion | flops 12582912 | bytes 34603008 | tf_op jit(solution)/shard_map/sub | solution.py:33
  191.2 9.8 %fusion.98 = f32[2,8,1024,128]{3,2,1,0:T(8,128)} fusion(f32[2,8,1024,128]{3,2,1,0:T(8,128)S(1)} %get-tuple-element.7), kind=kOutput, calls=%fused_computation.148 | convolution fusion | flops 3221454848 | bytes 16777216 | tf_op jit(solution)/shard_map/ub,...tb->...tu/dot_general | solution.py:47
  201.0 7.8 %fusion.96 = f32[2,8,1024,128]{3,2,1,0:T(8,128)S(1)} fusion(f32[2,8,1024,128]{3,2,1,0:T(8,128)S(1)} %get-tuple-element.8), kind=kOutput, calls=%fused_computation.146 | convolution fusion | flops 3221454848 | bytes 16777216 | tf_op jit(solution)/shard_map/ub,...tb->...tu/dot_general | solution.py:48
  208.8 11.4 %convolution_subtract_fusion = f32[2,8,1024,128]{3,2,1,0:T(8,128)} fusion(f32[2,8,1024,128]{3,2,1,0:T(8,128)} %fusion.98, f32[2,8,1024,128]{3,2,1,0:T(8,128)S(1)} %get-tuple-element.8), kind=kOutput, calls=%fused_computation.78 | convolution fusion | flops 3223568384 | bytes 25165824 | tf_op jit(solution)/shard_map/ub,...tb->...tu/dot_general | solution.py:47
  220.2 9.6 %convolution_add_fusion = f32[2,8,1024,128]{3,2,1,0:T(8,128)} fusion(f32[2,8,1024,128]{3,2,1,0:T(8,128)S(1)} %fusion.96, f32[2,8,1024,128]{3,2,1,0:T(8,128)S(1)} %get-tuple-element.7), kind=kOutput, calls=%fused_computation.77 | convolution fusion | flops 3223568384 | bytes 25165824 | tf_op jit(solution)/shard_map/ub,...tb->...tu/dot_general | solution.py:48
  229.7 4.2 multiply_subtract_fusion
  233.9 3.8 fusion.22
  237.7 3.8 fusion.20
  241.6 3.8 fusion.44
  245.5 5.2 %fusion.18 = (f32[8,128,1024]{1,2,0:T(8,128)S(1)}, f32[8,128,1024]{1,2,0:T(8,128)S(1)}) fusion(f32[8,1024,128]{2,1,0:T(8,128)S(1)} %fusion.44, f32[128,1024]{0,1:T(8,128)S(1)} %copy-done.7, f32[128,1024]{0,1:T(8,128)S(1)} %copy-done.6, f32[8,1024,128]{2,1,0:T(8,128)S(1)} %fusion.20, f32[1,8,1024,128]{3,2,1,0:T(8,128)S(1)} %get-tuple-element.9), kind=kOutput, calls=%fused_computation.52 | convolution fusion | flops 1618182144 | bytes 22020096 | tf_op jit(solution)/shard_map/bu,...tu->...tb/dot_general | solution.py:48
  250.7 7.0 %fusion.94 = f32[8,128,8,128]{3,1,2,0:T(8,128)S(1)} fusion(f32[8,128,8,128]{1,3,2,0:T(8,128)S(1)} %bitcast.227), kind=kOutput, calls=%fused_computation.144 | convolution fusion | flops 1610842112 | bytes 8388608 | tf_op jit(solution)/shard_map/bu,...tu->...tb/dot_general | solution.py:47
  257.7 7.3 %fusion.92 = f32[8,128,8,128]{3,1,2,0:T(8,128)S(1)} fusion(f32[8,128,8,128]{1,3,2,0:T(8,128)S(1)} %bitcast.229), kind=kOutput, calls=%fused_computation.142 | convolution fusion | flops 1610842112 | bytes 8388608 | tf_op jit(solution)/shard_map/bu,...tu->...tb/dot_general | solution.py:48
  265.0 7.1 %convolution_subtract_fusion.1 = f32[8,128,8,128]{3,1,2,0:T(8,128)S(1)} fusion(f32[8,128,8,128]{3,1,2,0:T(8,128)S(1)} %fusion.94, f32[8,128,8,128]{1,3,2,0:T(8,128)S(1)} %bitcast.230), kind=kOutput, calls=%fused_computation.82 | convolution fusion | flops 1611890688 | bytes 12582912 | tf_op jit(solution)/shard_map/bu,...tu->...tb/dot_general | solution.py:47
  272.1 7.3 %fusion.16 = (f32[8,128,128,8]{2,1,3,0:T(8,128)S(1)}, f32[8,128,128,8]{2,1,3,0:T(8,128)S(1)}) fusion(f32[8,128,8,128]{3,1,2,0:T(8,128)S(1)} %convolution_subtract_fusion.1, f32[128,8]{0,1:T(8,128)S(1)} %get-tuple-element.27, f32[128,8]{0,1:T(8,128)S(1)} %get-tuple-element.28, f32[8,128,8,128]{3,1,2,0:T(8,128)S(1)} %fusion.92, ...), kind=kOutput, calls=%fused_computation.46 | convolution fusion | flops 1618182144 | bytes 20979712 | tf_op jit(solution)/shard_map/bu,...tu->...tb/dot_general | solution.py:48
  279.4 6.6 %fusion.28 = f32[8,128,128,8]{2,3,1,0:T(8,128)S(1)} fusion(f32[8,128,128,8]{2,1,3,0:T(8,128)S(1)} %get-tuple-element.14), kind=kOutput, calls=%fused_computation.64 | convolution fusion | flops 100664192 | bytes 8388608 | tf_op jit(solution)/shard_map/kn,...n->...k/dot_general | solution.py:47
  286.0 6.9 %subtract_bitcast_fusion = f32[8,128,8,128]{3,2,1,0:T(8,128)} fusion(f32[8,128,128,8]{2,3,1,0:T(8,128)S(1)} %fusion.28, f32[8,128,128,8]{2,1,3,0:T(8,128)S(1)} %get-tuple-element.13), kind=kOutput, calls=%fused_computation.68 | convolution fusion | flops 101712768 | bytes 12582912 | tf_op jit(solution)/shard_map/kn,...n->...k/dot_general | solution.py:47
  292.9 5.4 %copy.65 = f32[8,128,8,128]{1,3,2,0:T(8,128)} copy(f32[8,128,8,128]{3,2,1,0:T(8,128)} %subtract_bitcast_fusion) | data formatting | bytes 8388608 | tf_op jit(solution)/shard_map/reshape | solution.py:104
  298.3 4.6 copy.91
  303.0 0.0 copy-start.4
  303.0 0.0 copy-start.8
  303.0 0.0 copy-start.12
  303.0 0.1 slice.32
  303.1 70.2 %all_to_all.13 = f32[8,8,8192]{2,0,1:T(8,128)S(1)} all-to-all(f32[8,8,8192]{2,0,1:T(8,128)S(1)} %bitcast.240), channel_id=1, replica_groups=mesh['seq'=8,'chan'=4] {'seq'}, dimensions={1} | all-to-all | bytes 4194304 | tf_op jit(solution)/shard_map/all_to_all | solution.py:119
  373.3 9.1 %convolution_bitcast_fusion = f32[256,8192]{0,1:T(8,128)} fusion(f32[256,64]{0,1:T(8,128)S(1)} %copy-done, f32[64,8192]{1,0:T(8,128)S(1)} %copy-done.8, f32[64,8192]{1,0:T(8,128)S(1)} %copy-done.4, f32[8,8,8192]{2,0,1:T(8,128)S(1)} %all_to_all.13, f32[64]{0:T(128)S(1)} %copy-done.12), kind=kOutput, calls=%fused_computation | convolution fusion | flops 1612709888 | bytes 14745856 | tf_op jit(solution)/shard_map/dot_general | solution.py:131
  382.4 9.0 %copy.66 = f32[256,8192]{1,0:T(8,128)} copy(f32[256,8192]{0,1:T(8,128)} %convolution_bitcast_fusion) | data formatting | bytes 16777216
  391.4 0.0 reduce-scatter.4.cloned.1.call-update
  391.4 70.6 %reduce-scatter.4.cloned.1.call-done = f32[64,8192]{1,0:T(8,128)} async-done(((f32[256,8192]{1,0:T(8,128)}), f32[64,8192]{1,0:T(8,128)}) %reduce-scatter.4.cloned.1.call-update) | async-done | bytes 2097168 | tf_op jit(solution)/shard_map/reduce_scatter | solution.py:130
  (32 shorter events, 0.2 us)
Async XLA Ops:
  6.5 366.8 %copy-start = (f32[256,64]{0,1:T(8,128)S(1)}, f32[256,64]{0,1:T(8,128)}, u32[]{:S(2)}) copy-start(f32[256,64]{0,1:T(8,128)} %param.13) | copy-start | bytes 196612
  6.5 12.7 %copy-start.3 = (f32[64,8192]{1,0:T(8,128)S(1)}, f32[64,8192]{1,0:T(8,128)}, u32[]{:S(2)}) copy-start(f32[64,8192]{1,0:T(8,128)} %param.9) | copy-start | bytes 6291460
  6.5 455.5 %reduce-scatter.4.cloned.1.call-start = ((), (), s32[]{:S(2)}) async-start(), calls=%async_computation.2 | async-start | bytes 10485760 | tf_op jit(solution)/shard_map/reduce_scatter | solution.py:130
  10.3 10.7 %copy-start.11 = (s32[1024]{0:T(1024)S(1)}, s32[1024]{0:T(1024)}, u32[]{:S(2)}) copy-start(s32[1024]{0:T(1024)} %constant.133.clone) | copy-start | bytes 12292
  10.3 26.9 %collective-permute-start = (f32[2,1,8,8192]{3,2,0,1:T(8,128)}, f32[2,1,8,8192]{3,2,0,1:T(8,128)}, u32[]{:S(2)}, u32[]{:S(2)}) collective-permute-start(f32[2,1,8,8192]{3,2,0,1:T(8,128)} %get-tuple-element.16), channel_id=1, source_target_pairs={{0,4},{4,0},{8,12},{12,8},{16,20},{20,16},{24,28},{28,24},{1,5},{5... | collective-permute-start | bytes 1572872 | tf_op jit(solution)/shard_map/ppermute | solution.py:21
  13.2 36.7 %collective-permute-start.1 = (f32[2,1,8,8192]{3,2,0,1:T(8,128)}, f32[2,1,8,8192]{3,2,0,1:T(8,128)}, u32[]{:S(2)}, u32[]{:S(2)}) collective-permute-start(f32[2,1,8,8192]{3,2,0,1:T(8,128)} %get-tuple-element.17), channel_id=1, source_target_pairs={{0,8},{4,12},{8,0},{12,4},{16,24},{20,28},{24,16},{28,20},{1,9},{5... | collective-permute-start | bytes 1572872 | tf_op jit(solution)/shard_map/ppermute | solution.py:21
  14.8 44.1 %collective-permute-start.2 = (f32[2,1,8,8192]{3,2,0,1:T(8,128)}, f32[2,1,8,8192]{3,2,0,1:T(8,128)}, u32[]{:S(2)}, u32[]{:S(2)}) collective-permute-start(f32[2,1,8,8192]{3,2,0,1:T(8,128)} %get-tuple-element.18), channel_id=1, source_target_pairs={{0,12},{4,8},{8,4},{12,0},{16,28},{20,24},{24,20},{28,16},{1,13},{... | collective-permute-start | bytes 1572872 | tf_op jit(solution)/shard_map/ppermute | solution.py:21
  14.8 45.1 %collective-permute-start.3 = (f32[2,1,8,8192]{3,2,0,1:T(8,128)}, f32[2,1,8,8192]{3,2,0,1:T(8,128)}, u32[]{:S(2)}, u32[]{:S(2)}) collective-permute-start(f32[2,1,8,8192]{3,2,0,1:T(8,128)} %get-tuple-element.19), channel_id=1, source_target_pairs={{0,16},{4,20},{8,24},{12,28},{16,0},{20,4},{24,8},{28,12},{1,17},{... | collective-permute-start | bytes 1572872 | tf_op jit(solution)/shard_map/ppermute | solution.py:21
  17.8 70.5 %collective-permute-start.4 = (f32[2,1,8,8192]{3,2,0,1:T(8,128)}, f32[2,1,8,8192]{3,2,0,1:T(8,128)}, u32[]{:S(2)}, u32[]{:S(2)}) collective-permute-start(f32[2,1,8,8192]{3,2,0,1:T(8,128)} %get-tuple-element.20), channel_id=1, source_target_pairs={{0,20},{4,16},{8,28},{12,24},{16,4},{20,0},{24,12},{28,8},{1,21},{... | collective-permute-start | bytes 1572872 | tf_op jit(solution)/shard_map/ppermute | solution.py:21
  23.1 1.6 copy-start.5
  28.2 8.9 %copy-start.10 = (f32[2,1,8,8192]{3,2,0,1:T(8,128)S(1)}, f32[2,1,8,8192]{3,2,0,1:T(8,128)}, u32[]{:S(2)}) copy-start(f32[2,1,8,8192]{3,2,0,1:T(8,128)} %fusion.71) | copy-start | bytes 1572868
  28.2 21.8 %copy-start.9 = (f32[2,1,8,8192]{3,2,0,1:T(8,128)S(1)}, f32[2,1,8,8192]{3,2,0,1:T(8,128)}, u32[]{:S(2)}) copy-start(f32[2,1,8,8192]{3,2,0,1:T(8,128)} %get-tuple-element.15) | copy-start | bytes 1572868
  37.1 52.3 %collective-permute-start.5 = (f32[2,1,8,8192]{3,2,0,1:T(8,128)S(1)}, f32[2,1,8,8192]{3,2,0,1:T(8,128)S(1)}, u32[]{:S(2)}, u32[]{:S(2)}) collective-permute-start(f32[2,1,8,8192]{3,2,0,1:T(8,128)S(1)} %copy-done.10), channel_id=1, source_target_pairs={{0,24},{4,28},{8,16},{12,20},{16,8},{20,12},{24,0},{28,4},{1,25},{... | collective-permute-start | bytes 1572872 | tf_op jit(solution)/shard_map/ppermute | solution.py:21
  50.0 39.5 %collective-permute-start.6 = (f32[2,1,8,8192]{3,2,0,1:T(8,128)S(1)}, f32[2,1,8,8192]{3,2,0,1:T(8,128)S(1)}, u32[]{:S(2)}, u32[]{:S(2)}) collective-permute-start(f32[2,1,8,8192]{3,2,0,1:T(8,128)S(1)} %copy-done.9), channel_id=1, source_target_pairs={{0,28},{4,24},{8,20},{12,16},{16,12},{20,8},{24,4},{28,0},{1,29},{... | collective-permute-start | bytes 1572872 | tf_op jit(solution)/shard_map/ppermute | solution.py:21
  103.7 12.3 %copy-start.1 = (f32[2,8,128,8,128]{4,3,2,1,0:T(8,128)S(1)}, f32[2,8,128,8,128]{4,3,2,1,0:T(8,128)}, u32[]{:S(2)}) copy-start(f32[2,8,128,8,128]{4,3,2,1,0:T(8,128)} %copy.64) | copy-start | bytes 25165828
  140.5 19.9 %slice-start = ((s8[8388608]{0:T(1024)(128)(4,1)}), s8[4194304]{0:T(1024)(128)(4,1)S(1)}, s32[]{:S(2)}) async-start(s8[8388608]{0:T(1024)(128)(4,1)} %bitcast.225), calls=%async_computation.3 | async-start | bytes 8388608
  151.6 8.9 %slice-start.1 = ((s8[8388608]{0:T(1024)(128)(4,1)}), s8[4194304]{0:T(1024)(128)(4,1)S(1)}, s32[]{:S(2)}) async-start(s8[8388608]{0:T(1024)(128)(4,1)} %bitcast.225), calls=%async_computation.4 | async-start | bytes 8388608
  220.2 9.6 %copy-start.2 = (f32[2,8,1024,128]{3,2,1,0:T(8,128)S(1)}, f32[2,8,1024,128]{3,2,1,0:T(8,128)}, u32[]{:S(2)}) copy-start(f32[2,8,1024,128]{3,2,1,0:T(8,128)} %convolution_subtract_fusion) | copy-start | bytes 25165828
  241.6 3.9 copy-start.6
  241.6 3.9 copy-start.7
  303.0 70.3 %copy-start.4 = (f32[64,8192]{1,0:T(8,128)S(1)}, f32[64,8192]{1,0:T(8,128)}, u32[]{:S(2)}) copy-start(f32[64,8192]{1,0:T(8,128)} %param.9) | copy-start | bytes 6291460
  303.0 70.3 %copy-start.8 = (f32[64,8192]{1,0:T(8,128)S(1)}, f32[64,8192]{1,0:T(8,128)}, u32[]{:S(2)}) copy-start(f32[64,8192]{1,0:T(8,128)} %param.10) | copy-start | bytes 6291460
  303.0 70.3 %copy-start.12 = (f32[64]{0:T(128)S(1)}, f32[64]{0:T(128)}, u32[]{:S(2)}) copy-start(f32[64]{0:T(128)} %param.12) | copy-start | bytes 772
Sparse Core Ops, SparseCore 0:
  391.5 70.4 reduce-scatter.3
